TPU v7x, 32 devices: a whole 2x2x4 slice. The times are simulated.
32 devices in a mesh: group: 2 (over core), ctx: 8 (over z, x), mp: 2 (over y).
Axes of the slice: x: 2, y: 2, z: 4, core: 2. Of those that a mesh axis runs over, the one named last changes fastest.
Arguments:
- token_ids: int32 [2, 1024], P('group', 'ctx'), may hold values from 0 to 127
- span_offset: int32 [1], replicated, may hold values from 0 to 3071
- shard_lengths: int32 [8], P('ctx'), may hold values from 1 to 384
- embed_table: bfloat16 [128, 2560], P(None, 'mp'), may hold values from -6 to 6
- norm_gain: bfloat16 [2560], P('mp'), may hold values from 0.25 to 1.75
- query_weight: bfloat16 [2560, 2560], P('mp'), may hold values from -0.25 to 0.25
- key_weight: bfloat16 [2560, 2560], P('mp'), may hold values from -0.25 to 0.25
- value_weight: bfloat16 [2560, 2560], P('mp'), may hold values from -0.125 to 0.125
- cache_keys: bfloat16 [3072, 2560], P('ctx', 'mp'), may hold values from -440 to 440
- cache_values: bfloat16 [3072, 2560], P('ctx', 'mp'), may hold values from -6 to 6
Outputs:
- attended: bfloat16 [2, 1024, 2560], P('group', 'ctx', 'mp')
All inputs are finite; a program needn't handle non-finite values.
Results may differ from a plain program's by a relative error of at most 0.012.
The roundings to bfloat16 on the way count: a program that leaves them out, or rounds other values in their place, can miss the bound.
Values may be sent and summed in bfloat16 or wider, within the bound.
A program may use at most 256 MiB of HBM per device.

v0:
```python
import math
import jax
import jax.numpy as jnp
from jax import lax
from jax.sharding import PartitionSpec as P

D = 2560
HD = 80
PROT = 256
STEPS = 4


def passed_along(value, axis, steps):
    count = lax.axis_size(axis)
    first, last = (max(0, -steps), min(count, count - steps))
    return lax.ppermute(value, axis, [(source, source + steps) for source in range(first, last)])


def rotate(values_in, positions):
    row_count = values_in.shape[0]
    head_count = values_in.shape[1] // HD
    quarter = HD // 4
    column = (positions % PROT).astype(jnp.float32)
    homolog = (positions // PROT).astype(jnp.float32)
    frequency = 10000.0 ** (-jnp.arange(quarter, dtype=jnp.float32) / quarter)
    angles = jnp.stack([column[:, None] * frequency, homolog[:, None] * frequency], 1)
    cosine = jnp.cos(angles)[:, None, :, None, :]
    sine_table = jnp.sin(angles)[:, None, :, None, :]
    pieces = values_in.reshape(row_count, head_count, 2, 2, quarter)
    partner = jnp.stack([-pieces[:, :, :, 1], pieces[:, :, :, 0]], 3)
    return (pieces * cosine + partner * sine_table).reshape(row_count, head_count * HD)


def block_partial(
    query_block, start, all_keys, all_values, live_length, span_base, cache_count, decoding
):
    block_rows = query_block.shape[0]
    head_count = query_block.shape[1] // HD
    key_slots = all_keys.shape[0]
    query_heads = query_block.reshape(block_rows, head_count, HD)
    key_heads = all_keys.reshape(key_slots, head_count, HD)
    value_heads = all_values.reshape(key_slots, head_count, HD)
    scores = jnp.einsum(
        "qhd,khd->hqk", query_heads, key_heads, preferred_element_type=jnp.float32
    ) * (1.0 / math.sqrt(HD))
    slot = jnp.arange(key_slots, dtype=jnp.int32)
    query_index = start + jnp.arange(block_rows, dtype=jnp.int32)
    cache_live = (slot < cache_count) & (slot < live_length)
    span_index = span_base + slot - cache_count
    span_seen = (slot >= cache_count)[None, :] & (
        decoding | (span_index[None, :] <= query_index[:, None])
    )
    visible = (cache_live[None, :] | span_seen)[None]
    block_max = jnp.max(jnp.where(visible, scores, -1e30), -1)
    weights = jnp.where(visible, jnp.exp(scores - block_max[..., None]), 0.0)
    block_sum = jnp.sum(weights, -1)
    block_acc = jnp.einsum(
        "hqk,khd->qhd",
        weights.astype(jnp.bfloat16),
        value_heads,
        preferred_element_type=jnp.float32,
    )
    return (block_max.T, block_sum.T, block_acc.reshape(block_rows, head_count * HD))


def local(
    token_ids,
    span_offset,
    shard_lengths,
    embed_table,
    norm_gain,
    query_weight,
    key_weight,
    value_weight,
    cache_keys,
    cache_values,
):
    token_row = token_ids[0]
    row_count = token_row.shape[0]
    ctx_count = lax.axis_size("ctx")
    ctx_index = lax.axis_index("ctx")
    decoding = lax.axis_index("group") == 1
    one_hot = (
        token_row[:, None] == jnp.arange(embed_table.shape[0], dtype=jnp.int32)[None, :]
    ).astype(jnp.bfloat16)
    embedded = jnp.dot(one_hot, embed_table, preferred_element_type=jnp.float32)
    square_sum = lax.psum(jnp.sum(embedded * embedded, 1), "mp")
    normal_rows = (
        embedded * lax.rsqrt(square_sum / D + 1e-05)[:, None] * norm_gain.astype(jnp.float32)
    ).astype(jnp.bfloat16)
    query_part = jnp.dot(normal_rows, query_weight, preferred_element_type=jnp.float32)
    key_part = jnp.dot(normal_rows, key_weight, preferred_element_type=jnp.float32)
    value_part = jnp.dot(normal_rows, value_weight, preferred_element_type=jnp.float32)
    query_full, key_full, value_full = (
        lax.psum_scatter(query_part, "mp", scatter_dimension=1, tiled=True),
        lax.psum_scatter(key_part, "mp", scatter_dimension=1, tiled=True),
        lax.psum_scatter(value_part, "mp", scatter_dimension=1, tiled=True),
    )
    offset_value = span_offset[0]
    local_iota = jnp.arange(row_count, dtype=jnp.int32)
    positions = jnp.where(
        decoding,
        offset_value + row_count * ctx_count + local_iota % STEPS,
        offset_value + ctx_index * row_count + local_iota,
    )
    queries = rotate(query_full, positions).astype(jnp.bfloat16)
    new_keys = rotate(key_full, positions).astype(jnp.bfloat16)
    new_values = value_full.astype(jnp.bfloat16)
    width = queries.shape[1]
    head_count = width // HD
    span_keys, span_values = passed_along((new_keys, new_values), "group", 1)
    block_keys = jnp.where(decoding, span_keys, new_keys)
    block_values = jnp.where(decoding, span_values, new_values)
    cache_count = cache_keys.shape[0]
    all_keys = jnp.concatenate([cache_keys, block_keys], 0)
    all_values = jnp.concatenate([cache_values, block_values], 0)
    live_length = shard_lengths[0]
    span_base = ctx_index * row_count
    gathered = lax.all_gather(queries, "ctx", axis=0, tiled=True)
    total = gathered.shape[0]
    block_rows = math.gcd(total, 512)
    block_count = total // block_rows
    block_starts = jnp.arange(block_count, dtype=jnp.int32) * block_rows

    def one_block(pair):
        return block_partial(
            pair[0], pair[1], all_keys, all_values, live_length, span_base, cache_count, decoding
        )

    maxima, totals, sums = lax.map(
        one_block, (gathered.reshape(block_count, block_rows, width), block_starts)
    )
    maxima = maxima.reshape(total, head_count)
    totals = totals.reshape(total, head_count)
    sums = sums.reshape(total, width)
    got_max, got_sum, got_acc = (
        lax.all_to_all(maxima[None], "ctx", split_axis=1, concat_axis=0, tiled=True),
        lax.all_to_all(totals[None], "ctx", split_axis=1, concat_axis=0, tiled=True),
        lax.all_to_all(sums[None], "ctx", split_axis=1, concat_axis=0, tiled=True),
    )
    whole_max = jnp.max(got_max, 0)
    rescale = jnp.exp(got_max - whole_max[None])
    whole_sum = jnp.sum(rescale * got_sum, 0)
    whole_acc = jnp.sum(got_acc * jnp.repeat(rescale, HD, axis=2), 0)
    cands = row_count // STEPS
    own_q = queries.reshape(cands, STEPS, head_count, HD)
    own_k = new_keys.reshape(cands, STEPS, head_count, HD)
    own_v = new_values.reshape(cands, STEPS, head_count, HD)
    own_scores = jnp.einsum("ashd,athd->ahst", own_q, own_k, preferred_element_type=jnp.float32) * (
        1.0 / math.sqrt(HD)
    )
    step_iota = jnp.arange(STEPS, dtype=jnp.int32)
    own_visible = (step_iota[None, :] <= step_iota[:, None]) & decoding
    own_max = jnp.max(jnp.where(own_visible, own_scores, -1e30), -1)
    final_max = jnp.maximum(whole_max, own_max.transpose(0, 2, 1).reshape(row_count, head_count))
    keep_old = jnp.exp(whole_max - final_max)
    final_cand = final_max.reshape(cands, STEPS, head_count).transpose(0, 2, 1)
    own_weights = jnp.where(own_visible, jnp.exp(own_scores - final_cand[..., None]), 0.0)
    own_sum = jnp.sum(own_weights, -1).transpose(0, 2, 1).reshape(row_count, head_count)
    own_acc = jnp.einsum(
        "ahst,athd->ashd",
        own_weights.astype(jnp.bfloat16),
        own_v,
        preferred_element_type=jnp.float32,
    ).reshape(row_count, width)
    numer = whole_acc * jnp.repeat(keep_old, HD, axis=1) + own_acc
    denom = whole_sum * keep_old + own_sum
    output = numer / jnp.repeat(denom, HD, axis=1)
    return output.astype(jnp.bfloat16)[None]


def solution(mesh):
    placed = (
        P("group", "ctx"),
        P(),
        P("ctx"),
        P(None, "mp"),
        P("mp"),
        P("mp", None),
        P("mp", None),
        P("mp", None),
        P("ctx", "mp"),
        P("ctx", "mp"),
    )
    return jax.shard_map(
        local, mesh=mesh, in_specs=placed, out_specs=P("group", "ctx", "mp"), check_vma=False
    )
```

profile of v0, /device:TPU:0, one launch (start us, length us, event | category | flops | bytes accessed | tf_op | source)
XLA Modules:
  0.0 382.4 jit_solution(8588172545605878299)
XLA Ops:
  8.5 5.9 %psum.7 = f32[128]{0:T(128)S(1)} all-reduce(f32[128]{0:T(128)S(1)} %get-tuple-element.257), channel_id=1, replica_groups=mesh['group'=2,'ctx'=8,'mp'=2] {'mp'}, use_global_device_ids=true, to_apply=%region_1.0 | all-reduce | flops 128 | bytes 1024 | tf_op jit(solution)/shard_map/psum | solution.py:87
  14.6 5.0 %fusion.29 = f32[128,2560]{1,0:T(8,128)} fusion(bf16[128,1280]{1,0:T(8,128)(2,1)S(1)} %multiply_convert_fusion, bf16[1280,2560]{1,0:T(8,128)(2,1)} %param.18), kind=kOutput, calls=%fused_computation.76 | convolution fusion | flops 838860800 | bytes 8192000 | tf_op jit(solution)/shard_map/dot_general | solution.py:92
  19.6 5.0 %fusion.28 = f32[128,2560]{1,0:T(8,128)} fusion(bf16[128,1280]{1,0:T(8,128)(2,1)S(1)} %multiply_convert_fusion, bf16[1280,2560]{1,0:T(8,128)(2,1)} %param.17), kind=kOutput, calls=%fused_computation.75 | convolution fusion | flops 838860800 | bytes 8192000 | tf_op jit(solution)/shard_map/dot_general | solution.py:91
  24.7 5.0 %fusion.30 = f32[128,2560]{1,0:T(8,128)} fusion(bf16[128,1280]{1,0:T(8,128)(2,1)S(1)} %multiply_convert_fusion, bf16[1280,2560]{1,0:T(8,128)(2,1)} %param.19), kind=kOutput, calls=%fused_computation.77 | convolution fusion | flops 838860800 | bytes 8192000 | tf_op jit(solution)/shard_map/dot_general | solution.py:93
  31.9 12.9 %reduce-scatter.6.cloned.1.call-done = f32[128,1280]{1,0:T(8,128)} async-done(((f32[128,2560]{1,0:T(8,128)}), f32[128,1280]{1,0:T(8,128)}) %reduce-scatter.6.cloned.1.call-update) | async-done | bytes 655376 | tf_op jit(solution)/shard_map/reduce_scatter | solution.py:96
  46.2 24.2 %reduce-scatter.4.cloned.1.call-done = f32[128,1280]{1,0:T(8,128)} async-done(((f32[128,2560]{1,0:T(8,128)}), f32[128,1280]{1,0:T(8,128)}) %reduce-scatter.4.cloned.1.call-update) | async-done | bytes 655376 | tf_op jit(solution)/shard_map/reduce_scatter | solution.py:95
  73.4 2.6 add_convert_fusion.1
  81.0 14.9 %reduce-scatter.8.cloned.1.call-done = f32[128,1280]{1,0:T(8,128)} async-done(((f32[128,2560]{1,0:T(8,128)}), f32[128,1280]{1,0:T(8,128)}) %reduce-scatter.8.cloned.1.call-update) | async-done | bytes 655376 | tf_op jit(solution)/shard_map/reduce_scatter | solution.py:97
  97.0 2.3 collective-permute-start.1
  100.0 1.9 broadcast_select_fusion
  105.4 46.9 %all-gather.2.cloned.1.call-done = bf16[1024,1280]{1,0:T(8,128)(2,1)} async-done(((bf16[128,1280]{1,0:T(8,128)(2,1)}), bf16[1024,1280]{1,0:T(8,128)(2,1)}) %all-gather.2.cloned.1.call-update) | async-done | bytes 2621456 | tf_op jit(solution)/shard_map/all_gather | solution.py:119
  152.3 70.8 %while.16 = (s32[]{:T(128)}, f32[2,512,16]{1,2,0:T(8,128)S(1)}, f32[2,512,16]{1,2,0:T(8,128)S(1)}, f32[2,512,1280]{2,1,0:T(8,128)}, s32[]{:T(128)}, /*index=5*/p...) while((s32[]{:T(128)}, f32[2,512,16]{1,2,0:T(8,128)S(1)}, ...), condition=%wide.region_8.9_spmd, body=%wide.region_5.8_spmd.sunk | while | flops 1389350400 | bytes 79177912 | solution.py:130
  156.7 8.8 %select_reduce_fusion.3 = (f32[16,512]{1,0:T(8,128)S(1)}, f32[16,512,512]{1,2,0:T(8,128)}) fusion(pred[512,512]{0,1:T(8,128)(4,1)S(1)} %and_or_fusion.2, bf16[512,16,80]{0,2,1:T(8,128)(2,1)S(1)} %bitcast.97, bf16[512,16,80]{0,2,1:T(8,128)(2,1)} %bitcast.99), kind=kOutput, calls=%fused_computation.1.clone.1 | convolution fusion | flops 683663360 | bytes 19693568 | tf_op jit(solution)/shard_map/while/body/eval_jaxpr/qhd,khd->hqk/dot_general | solution.py:43
  165.5 9.3 %fusion.54 = f32[16,512]{1,0:T(8,128)S(1)} fusion(f32[16,512,512]{1,2,0:T(8,128)} %get-tuple-element.334, f32[16,512]{1,0:T(8,128)S(1)} %get-tuple-element.335, pred[512,512]{0,1:T(8,128)(4,1)S(1)} %and_or_fusion.2), kind=kLoop, calls=%fused_computation.3.clone.1 | loop fusion | flops 16769024 | bytes 17104896 | tf_op jit(solution)/shard_map/while/body/eval_jaxpr/reduce_sum | solution.py:56
  174.7 9.2 %fusion.55 = f32[16,512,80]{1,2,0:T(8,128)} fusion(bf16[512,16,80]{0,2,1:T(8,128)(2,1)S(1)} %bitcast.111, f32[16,512,512]{1,2,0:T(8,128)} %get-tuple-element.334, f32[16,512]{1,0:T(8,128)S(1)} %get-tuple-element.335, pred[512,512]{0,1:T(8,128)(4,1)S(1)} %and_or_fusion.2), kind=kOutput, calls=%fused_computation.4.clone.1 | convolution fusion | flops 687865856 | bytes 21004288 | tf_op jit(solution)/shard_map/while/body/eval_jaxpr/hqk,khd->qhd/dot_general | solution.py:57
  183.9 2.1 copy.222
  192.1 8.8 %select_reduce_fusion.3 = (f32[16,512]{1,0:T(8,128)S(1)}, f32[16,512,512]{1,2,0:T(8,128)}) fusion(pred[512,512]{0,1:T(8,128)(4,1)S(1)} %and_or_fusion.2, bf16[512,16,80]{0,2,1:T(8,128)(2,1)S(1)} %bitcast.97, bf16[512,16,80]{0,2,1:T(8,128)(2,1)} %bitcast.99), kind=kOutput, calls=%fused_computation.1.clone.1 | convolution fusion | flops 683663360 | bytes 19693568 | tf_op jit(solution)/shard_map/while/body/eval_jaxpr/qhd,khd->hqk/dot_general | solution.py:43
  200.8 9.3 %fusion.54 = f32[16,512]{1,0:T(8,128)S(1)} fusion(f32[16,512,512]{1,2,0:T(8,128)} %get-tuple-element.334, f32[16,512]{1,0:T(8,128)S(1)} %get-tuple-element.335, pred[512,512]{0,1:T(8,128)(4,1)S(1)} %and_or_fusion.2), kind=kLoop, calls=%fused_computation.3.clone.1 | loop fusion | flops 16769024 | bytes 17104896 | tf_op jit(solution)/shard_map/while/body/eval_jaxpr/reduce_sum | solution.py:56
  210.1 9.2 %fusion.55 = f32[16,512,80]{1,2,0:T(8,128)} fusion(bf16[512,16,80]{0,2,1:T(8,128)(2,1)S(1)} %bitcast.111, f32[16,512,512]{1,2,0:T(8,128)} %get-tuple-element.334, f32[16,512]{1,0:T(8,128)S(1)} %get-tuple-element.335, pred[512,512]{0,1:T(8,128)(4,1)S(1)} %and_or_fusion.2), kind=kOutput, calls=%fused_computation.4.clone.1 | convolution fusion | flops 687865856 | bytes 21004288 | tf_op jit(solution)/shard_map/while/body/eval_jaxpr/hqk,khd->qhd/dot_general | solution.py:57
  219.3 2.1 copy.222
  221.4 1.7 constant_dynamic-update-slice_fusion.2
  223.9 2.0 reduce
  226.7 3.6 all-to-all-start.1
  230.5 2.0 reduce.2
  233.4 3.6 all-to-all-done.1
  236.9 3.3 all-to-all-start.2
  240.3 10.2 %copy.168 = f32[1,1024,1280]{2,0,1:T(1,128)} copy(f32[1,1024,1280]{2,1,0:T(8,128)} %bitcast.103) | data formatting | bytes 10485760 | tf_op jit(solution)/shard_map/broadcast_in_dim;reshape | solution.py:139
  250.5 6.1 %all-to-all-start = ((f32[1,1024,1280]{2,0,1:T(1,128)}), f32[1,1024,1280]{2,0,1:T(1,128)}, u32[]{:S(2)}, u32[]{:S(2)}) async-start(f32[1,1024,1280]{2,0,1:T(1,128)} %copy.168), calls=%async_computation.3 | async-start | bytes 10485760 | tf_op jit(solution)/shard_map/all_to_all | solution.py:139
  268.6 2.6 broadcast_in_dim.99
  271.2 5.9 %copy.174 = f32[8,128,1280]{2,1,0:T(8,128)} copy(f32[8,128,1280]{1,2,0:T(8,128)} %bitcast.101) | data formatting | bytes 10485760 | tf_op jit(solution)/shard_map/reshape | solution.py:144
  277.1 92.9 %all-to-all-done = f32[1,1024,1280]{2,0,1:T(1,128)} async-done(((f32[1,1024,1280]{2,0,1:T(1,128)}), f32[1,1024,1280]{2,0,1:T(1,128)}, u32[]{:S(2)}, u32[]{:S(2)}) %all-to-all-start) | async-done | bytes 5242912 | tf_op jit(solution)/shard_map/all_to_all | solution.py:139
  370.0 3.0 copy.203
  (122 shorter events, 46.0 us)
Async XLA Ops:
  6.5 1.0 copy-start
  6.5 38.2 %reduce-scatter.6.cloned.1.call-start = ((), (), s32[]{:S(2)}) async-start(), calls=%async_computation.8 | async-start | bytes 1966080 | tf_op jit(solution)/shard_map/reduce_scatter | solution.py:96
  19.6 50.7 %reduce-scatter.4.cloned.1.call-start = ((), (), s32[]{:S(2)}) async-start(), calls=%async_computation.6 | async-start | bytes 1966080 | tf_op jit(solution)/shard_map/reduce_scatter | solution.py:95
  24.6 71.3 %reduce-scatter.8.cloned.1.call-start = ((), (), s32[]{:S(2)}) async-start(), calls=%async_computation.9 | async-start | bytes 1966080 | tf_op jit(solution)/shard_map/reduce_scatter | solution.py:97
  29.7 122.6 %all-gather.2.cloned.1.call-start = ((), (), s32[]{:S(2)}) async-start(), calls=%async_computation.7 | async-start | bytes 2949120 | tf_op jit(solution)/shard_map/all_gather | solution.py:119
  76.0 23.3 %collective-permute-start = (bf16[128,1280]{1,0:T(8,128)(2,1)S(1)}, bf16[128,1280]{1,0:T(8,128)(2,1)S(1)}, u32[]{:S(2)}, u32[]{:S(2)}) collective-permute-start(bf16[128,1280]{1,0:T(8,128)(2,1)S(1)} %get-tuple-element.248), channel_id=1, source_target_pairs={{0,16},{1,17},{2,18},{3,19},{4,20},{5,21},{6,22},{7,23},{8,24},{9,... | collective-permute-start | bytes 983048 | tf_op jit(solution)/shard_map/ppermute | solution.py:16
  97.0 55.3 %copy-start.5 = (bf16[128,1280]{1,0:T(8,128)(2,1)}, bf16[128,1280]{1,0:T(8,128)(2,1)S(1)}, u32[]{:S(2)}) copy-start(bf16[128,1280]{1,0:T(8,128)(2,1)S(1)} %convert_element_type.57) | copy-start | bytes 983044
  97.0 2.9 collective-permute-start.1
  165.5 9.3 %copy-start.4 = (bf16[512,1280]{0,1:T(8,128)(2,1)S(1)}, bf16[512,1280]{0,1:T(8,128)(2,1)}, u32[]{:S(2)}) copy-start(bf16[512,1280]{0,1:T(8,128)(2,1)} %get-tuple-element.372) | copy-start | bytes 3932164 | tf_op jit(solution)/shard_map/while
  200.8 9.3 %copy-start.4 = (bf16[512,1280]{0,1:T(8,128)(2,1)S(1)}, bf16[512,1280]{0,1:T(8,128)(2,1)}, u32[]{:S(2)}) copy-start(bf16[512,1280]{0,1:T(8,128)(2,1)} %get-tuple-element.372) | copy-start | bytes 3932164 | tf_op jit(solution)/shard_map/while
  226.7 10.2 %all-to-all-start.1 = ((f32[8,1,2048]{2,1,0:T(1,128)}), f32[8,1,2048]{2,1,0:T(1,128)S(1)}, u32[]{:S(2)}, u32[]{:S(2)}) async-start(f32[8,1,2048]{2,1,0:T(1,128)} %reshape.390), calls=%async_computation.4 | async-start | bytes 131072 | tf_op jit(solution)/shard_map/all_to_all | solution.py:137
  236.9 13.6 %all-to-all-start.2 = ((f32[8,1,2048]{2,1,0:T(1,128)}), f32[8,1,2048]{2,1,0:T(1,128)S(1)}, u32[]{:S(2)}, u32[]{:S(2)}) async-start(f32[8,1,2048]{2,1,0:T(1,128)} %reshape.392), calls=%async_computation.5 | async-start | bytes 131072 | tf_op jit(solution)/shard_map/all_to_all | solution.py:138
  250.5 6.9 %copy-start.3 = (bf16[128,1280]{1,0:T(8,128)(2,1)S(1)}, bf16[128,1280]{1,0:T(8,128)(2,1)}, u32[]{:S(2)}) copy-start(bf16[128,1280]{1,0:T(8,128)(2,1)} %get-tuple-element.247) | copy-start | bytes 983044
  250.5 7.7 %copy-start.6 = (bf16[128,1280]{1,0:T(8,128)(2,1)S(1)}, bf16[128,1280]{1,0:T(8,128)(2,1)}, u32[]{:S(2)}) copy-start(bf16[128,1280]{1,0:T(8,128)(2,1)} %copy-done.5) | copy-start | bytes 983044
  250.5 119.5 %all-to-all-start = ((f32[1,1024,1280]{2,0,1:T(1,128)}), f32[1,1024,1280]{2,0,1:T(1,128)}, u32[]{:S(2)}, u32[]{:S(2)}) async-start(f32[1,1024,1280]{2,0,1:T(1,128)} %copy.168), calls=%async_computation.3 | async-start | bytes 10485760 | tf_op jit(solution)/shard_map/all_to_all | solution.py:139
  370.0 4.0 %copy-start.2 = (f32[8,128,1280]{2,1,0:T(8,128)S(1)}, f32[8,128,1280]{2,1,0:T(8,128)}, u32[]{:S(2)}) copy-start(f32[8,128,1280]{2,1,0:T(8,128)} %copy.174) | copy-start | bytes 15728644
  373.0 2.9 copy-start.1
Sparse Core Ops, SparseCore 0:
  19.7 25.0 reduce-scatter.5
  47.0 23.2 reduce-scatter.3
  72.6 23.2 reduce-scatter.7
  97.9 54.3 all-gather.1
where the time goes:
time: 384 us; the launch traced here: 382 us
  waiting for transfers between devices  196 us (51%)
  local copies, waits for them, and re-layouts  57.1 us (15%)
  matrix products  53.2 us (14%)
  other arithmetic  38.9 us (10%)
  starting transfers between devices  17 us (4%)
  between operations  14.2 us (4%)
  blocking collectives  5.9 us (2%)
    all_to_all x1, waiting for transfers between devices, local(): lax.all_to_all(sums[None], 'ctx', split_axis=1, concat_axis=0, tiled=True)  92.9 us
    all_gather x1, waiting for transfers between devices, local(): gathered = lax.all_gather(queries, 'ctx', axis=0, tiled=True)  46.9 us
    reduce_scatter x1, waiting for transfers between devices, local(): lax.psum_scatter(query_part, 'mp', scatter_dimension=1, tiled=True)  24.2 us
    reduce_sum x2, other arithmetic, block_partial(): block_sum = jnp.sum(weights, -1)  18.5 us
    dot_general x2, matrix products, block_partial(): jnp.einsum('hqk,khd->qhd', weights.astype(jnp.bfloat16), value_heads, pre...  18.3 us
    dot_general x2, matrix products, block_partial(): jnp.einsum('qhd,khd->hqk', query_heads, key_heads, preferred_element_type...  17.6 us
    reduce_scatter x1, waiting for transfers between devices, local(): lax.psum_scatter(value_part, 'mp', scatter_dimension=1, tiled=True)  14.9 us
    reduce_scatter x1, waiting for transfers between devices, local(): lax.psum_scatter(key_part, 'mp', scatter_dimension=1, tiled=True)  12.9 us
  transfers between devices with their start and end apart: 9, of which 7 were waited for; matrix products, arithmetic and copies ran while one was open for 16% of the time, Pallas kernels for 0%

commit v1 on v0

--- a/solution.py
+++ b/solution.py
@@ -116,7 +116,12 @@
     all_values = jnp.concatenate([cache_values, block_values], 0)
     live_length = shard_lengths[0]
     span_base = ctx_index * row_count
-    gathered = lax.all_gather(queries, "ctx", axis=0, tiled=True)
+    ring = [queries]
+    for hop in range(7):
+        ring.append(lax.ppermute(ring[-1], "ctx", [(dev, (dev + 1) % 8) for dev in range(8)]))
+    gathered = jnp.roll(
+        jnp.concatenate(ring[::-1], axis=0), (lax.axis_index("ctx") + 1) * ring[0].shape[0], axis=0
+    )
     total = gathered.shape[0]
     block_rows = math.gcd(total, 512)
     block_count = total // block_rows

time: 384 us -> 391 us (1.018); the launches traced: 382 us -> 384 us
  waiting for transfers between devices: 196 us -> 182 us
  local copies, waits for them, and re-layouts: 57.1 us -> 68.8 us
    ppermute x0 -> x7, waiting for transfers between devices: none -> 57.3 us  [local(): lax.ppermute(ring[-1], 'ctx', [(dev, (dev + 1) % 8) for dev in range(8)])]
    all_gather x1 -> x0, waiting for transfers between devices: 46.9 us -> none  [local(): gathered = lax.all_gather(queries, 'ctx', axis=0, tiled=True)]
    reduce_scatter x1, waiting for transfers between devices: 14.9 us -> 0.02 us  [local(): lax.psum_scatter(value_part, 'mp', scatter_dimension=1, tiled=True)]
    all_to_all x1, waiting for transfers between devices: 92.9 us -> 83.8 us  [local(): lax.all_to_all(sums[None], 'ctx', split_axis=1, concat_axis=0, tiled=True)]
    unnamed x22 -> x47, local copies, waits for them, and re-layouts: 11.9 us -> 20 us
  transfers between devices with their start and end apart: 9 -> 15, of which waited for: 7 -> 11; matrix products, arithmetic and copies ran while one was open for 16% -> 17% of each run, Pallas kernels for 0% -> 0%
where the time goes in v1:
time: 391 us; the launch traced here: 384 us
  waiting for transfers between devices  182 us (47%)
  local copies, waits for them, and re-layouts  68.8 us (18%)
  matrix products  54.2 us (14%)
  other arithmetic  39.1 us (10%)
  starting transfers between devices  19.3 us (5%)
  between operations  14.6 us (4%)
  blocking collectives  5.9 us (2%)
    all_to_all x1, waiting for transfers between devices, local(): lax.all_to_all(sums[None], 'ctx', split_axis=1, concat_axis=0, tiled=True)  83.8 us
    ppermute x7, waiting for transfers between devices, local(): lax.ppermute(ring[-1], 'ctx', [(dev, (dev + 1) % 8) for dev in range(8)])  57.3 us
    reduce_scatter x1, waiting for transfers between devices, local(): lax.psum_scatter(query_part, 'mp', scatter_dimension=1, tiled=True)  24.2 us
    unnamed x47, local copies, waits for them, and re-layouts  20 us
    reduce_sum x2, other arithmetic, block_partial(): block_sum = jnp.sum(weights, -1)  18.5 us
    dot_general x2, matrix products, block_partial(): jnp.einsum('hqk,khd->qhd', weights.astype(jnp.bfloat16), value_heads, pre...  18.3 us
    dot_general x2, matrix products, block_partial(): jnp.einsum('qhd,khd->hqk', query_heads, key_heads, preferred_element_type...  17.6 us
    reduce_scatter x1, waiting for transfers between devices, local(): lax.psum_scatter(key_part, 'mp', scatter_dimension=1, tiled=True)  13 us
  transfers between devices with their start and end apart: 15, of which 11 were waited for; matrix products, arithmetic and copies ran while one was open for 17% of the time, Pallas kernels for 0%

profile of v1, /device:TPU:0, one launch (start us, length us, event | category | flops | bytes accessed | tf_op | source)
XLA Modules:
  0.0 384.2 jit_solution(4868836382360753540)
XLA Ops:
  8.5 5.9 %psum.7 = f32[128]{0:T(128)S(1)} all-reduce(f32[128]{0:T(128)S(1)} %get-tuple-element.246), channel_id=1, replica_groups=mesh['group'=2,'ctx'=8,'mp'=2] {'mp'}, use_global_device_ids=true, to_apply=%region_1.0 | all-reduce | flops 128 | bytes 1024 | tf_op jit(solution)/shard_map/psum | solution.py:87
  14.6 5.0 %fusion.29 = f32[128,2560]{1,0:T(8,128)} fusion(bf16[128,1280]{1,0:T(8,128)(2,1)S(1)} %multiply_convert_fusion, bf16[1280,2560]{1,0:T(8,128)(2,1)} %param.18), kind=kOutput, calls=%fused_computation.93 | convolution fusion | flops 838860800 | bytes 8192000 | tf_op jit(solution)/shard_map/dot_general | solution.py:92
  19.6 5.0 %fusion.28 = f32[128,2560]{1,0:T(8,128)} fusion(bf16[128,1280]{1,0:T(8,128)(2,1)S(1)} %multiply_convert_fusion, bf16[1280,2560]{1,0:T(8,128)(2,1)} %param.17), kind=kOutput, calls=%fused_computation.92 | convolution fusion | flops 838860800 | bytes 8192000 | tf_op jit(solution)/shard_map/dot_general | solution.py:91
  24.7 5.0 %fusion.30 = f32[128,2560]{1,0:T(8,128)} fusion(bf16[128,1280]{1,0:T(8,128)(2,1)S(1)} %multiply_convert_fusion, bf16[1280,2560]{1,0:T(8,128)(2,1)} %param.19), kind=kOutput, calls=%fused_computation.94 | convolution fusion | flops 838860800 | bytes 8192000 | tf_op jit(solution)/shard_map/dot_general | solution.py:93
  31.8 13.0 %reduce-scatter.6.cloned.1.call-done = f32[128,1280]{1,0:T(8,128)} async-done(((f32[128,2560]{1,0:T(8,128)}), f32[128,1280]{1,0:T(8,128)}) %reduce-scatter.6.cloned.1.call-update) | async-done | bytes 655376 | tf_op jit(solution)/shard_map/reduce_scatter | solution.py:96
  46.2 24.2 %reduce-scatter.4.cloned.1.call-done = f32[128,1280]{1,0:T(8,128)} async-done(((f32[128,2560]{1,0:T(8,128)}), f32[128,1280]{1,0:T(8,128)}) %reduce-scatter.4.cloned.1.call-update) | async-done | bytes 655376 | tf_op jit(solution)/shard_map/reduce_scatter | solution.py:95
  76.9 10.5 %collective-permute-done = bf16[128,1280]{1,0:T(8,128)(2,1)S(1)} collective-permute-done((bf16[128,1280]{1,0:T(8,128)(2,1)S(1)}, bf16[128,1280]{1,0:T(8,128)(2,1)S(1)}, u32[]{:S(2)}, u32[]{:S(2)}) %collective-permute-start) | collective-permute-done | bytes 327712 | tf_op jit(solution)/shard_map/ppermute | solution.py:121
  87.4 11.1 %collective-permute-done.1 = bf16[128,1280]{1,0:T(8,128)(2,1)S(1)} collective-permute-done((bf16[128,1280]{1,0:T(8,128)(2,1)S(1)}, bf16[128,1280]{1,0:T(8,128)(2,1)S(1)}, u32[]{:S(2)}, u32[]{:S(2)}) %collective-permute-start.1) | collective-permute-done | bytes 327712 | tf_op jit(solution)/shard_map/ppermute | solution.py:121
  98.5 10.3 %collective-permute-done.2 = bf16[128,1280]{1,0:T(8,128)(2,1)S(1)} collective-permute-done((bf16[128,1280]{1,0:T(8,128)(2,1)S(1)}, bf16[128,1280]{1,0:T(8,128)(2,1)S(1)}, u32[]{:S(2)}, u32[]{:S(2)}) %collective-permute-start.2) | collective-permute-done | bytes 327712 | tf_op jit(solution)/shard_map/ppermute | solution.py:121
  108.8 2.0 collective-permute-start.7
  115.9 2.0 collective-permute-start.8
  118.9 9.8 %collective-permute-done.4 = bf16[128,1280]{1,0:T(8,128)(2,1)} collective-permute-done((bf16[128,1280]{1,0:T(8,128)(2,1)}, bf16[128,1280]{1,0:T(8,128)(2,1)}, u32[]{:S(2)}, u32[]{:S(2)}) %collective-permute-start.4) | collective-permute-done | bytes 327712 | tf_op jit(solution)/shard_map/ppermute | solution.py:121
  130.6 8.5 %collective-permute-done.5 = bf16[128,1280]{1,0:T(8,128)(2,1)} collective-permute-done((bf16[128,1280]{1,0:T(8,128)(2,1)}, bf16[128,1280]{1,0:T(8,128)(2,1)}, u32[]{:S(2)}, u32[]{:S(2)}) %collective-permute-start.5) | collective-permute-done | bytes 327712 | tf_op jit(solution)/shard_map/ppermute | solution.py:121
  143.3 6.4 %collective-permute-done.6 = bf16[128,1280]{1,0:T(8,128)(2,1)} collective-permute-done((bf16[128,1280]{1,0:T(8,128)(2,1)}, bf16[128,1280]{1,0:T(8,128)(2,1)}, u32[]{:S(2)}, u32[]{:S(2)}) %collective-permute-start.6) | collective-permute-done | bytes 327712 | tf_op jit(solution)/shard_map/ppermute | solution.py:121
  159.6 71.0 %while.16 = (s32[]{:T(128)}, f32[2,512,16]{1,2,0:T(8,128)S(1)}, f32[2,512,16]{1,2,0:T(8,128)S(1)}, f32[2,512,1280]{2,1,0:T(8,128)}, s32[]{:T(128)}, /*index=5*/p...) while((s32[]{:T(128)}, f32[2,512,16]{1,2,0:T(8,128)S(1)}, ...), condition=%wide.region_8.9_spmd, body=%wide.region_5.8_spmd.sunk | while | flops 1389350400 | bytes 79177912 | solution.py:135
  164.0 8.8 %select_reduce_fusion.3 = (f32[16,512]{1,0:T(8,128)S(1)}, f32[16,512,512]{1,2,0:T(8,128)}) fusion(pred[512,512]{0,1:T(8,128)(4,1)S(1)} %and_or_fusion.2, bf16[512,16,80]{0,2,1:T(8,128)(2,1)S(1)} %bitcast.97, bf16[512,16,80]{0,2,1:T(8,128)(2,1)} %bitcast.99), kind=kOutput, calls=%fused_computation.1.clone.1 | convolution fusion | flops 683663360 | bytes 19693568 | tf_op jit(solution)/shard_map/while/body/eval_jaxpr/qhd,khd->hqk/dot_general | solution.py:43
  172.8 9.3 %fusion.54 = f32[16,512]{1,0:T(8,128)S(1)} fusion(f32[16,512,512]{1,2,0:T(8,128)} %get-tuple-element.323, f32[16,512]{1,0:T(8,128)S(1)} %get-tuple-element.324, pred[512,512]{0,1:T(8,128)(4,1)S(1)} %and_or_fusion.2), kind=kLoop, calls=%fused_computation.3.clone.1 | loop fusion | flops 16769024 | bytes 17104896 | tf_op jit(solution)/shard_map/while/body/eval_jaxpr/reduce_sum | solution.py:56
  182.1 9.1 %fusion.55 = f32[16,512,80]{1,2,0:T(8,128)} fusion(bf16[512,16,80]{0,2,1:T(8,128)(2,1)S(1)} %bitcast.111, f32[16,512,512]{1,2,0:T(8,128)} %get-tuple-element.323, f32[16,512]{1,0:T(8,128)S(1)} %get-tuple-element.324, pred[512,512]{0,1:T(8,128)(4,1)S(1)} %and_or_fusion.2), kind=kOutput, calls=%fused_computation.4.clone.1 | convolution fusion | flops 687865856 | bytes 21004288 | tf_op jit(solution)/shard_map/while/body/eval_jaxpr/hqk,khd->qhd/dot_general | solution.py:57
  191.2 2.1 copy.221
  199.5 8.8 %select_reduce_fusion.3 = (f32[16,512]{1,0:T(8,128)S(1)}, f32[16,512,512]{1,2,0:T(8,128)}) fusion(pred[512,512]{0,1:T(8,128)(4,1)S(1)} %and_or_fusion.2, bf16[512,16,80]{0,2,1:T(8,128)(2,1)S(1)} %bitcast.97, bf16[512,16,80]{0,2,1:T(8,128)(2,1)} %bitcast.99), kind=kOutput, calls=%fused_computation.1.clone.1 | convolution fusion | flops 683663360 | bytes 19693568 | tf_op jit(solution)/shard_map/while/body/eval_jaxpr/qhd,khd->hqk/dot_general | solution.py:43
  208.3 9.3 %fusion.54 = f32[16,512]{1,0:T(8,128)S(1)} fusion(f32[16,512,512]{1,2,0:T(8,128)} %get-tuple-element.323, f32[16,512]{1,0:T(8,128)S(1)} %get-tuple-element.324, pred[512,512]{0,1:T(8,128)(4,1)S(1)} %and_or_fusion.2), kind=kLoop, calls=%fused_computation.3.clone.1 | loop fusion | flops 16769024 | bytes 17104896 | tf_op jit(solution)/shard_map/while/body/eval_jaxpr/reduce_sum | solution.py:56
  217.6 9.1 %fusion.55 = f32[16,512,80]{1,2,0:T(8,128)} fusion(bf16[512,16,80]{0,2,1:T(8,128)(2,1)S(1)} %bitcast.111, f32[16,512,512]{1,2,0:T(8,128)} %get-tuple-element.323, f32[16,512]{1,0:T(8,128)S(1)} %get-tuple-element.324, pred[512,512]{0,1:T(8,128)(4,1)S(1)} %and_or_fusion.2), kind=kOutput, calls=%fused_computation.4.clone.1 | convolution fusion | flops 687865856 | bytes 21004288 | tf_op jit(solution)/shard_map/while/body/eval_jaxpr/hqk,khd->qhd/dot_general | solution.py:57
  226.7 2.1 copy.221
  234.2 3.5 all-to-all-start.1
  240.8 3.8 all-to-all-done.1
  244.6 3.3 all-to-all-start.2
  247.9 10.2 %copy.167 = f32[1,1024,1280]{2,0,1:T(1,128)} copy(f32[1,1024,1280]{2,1,0:T(8,128)} %bitcast.103) | data formatting | bytes 10485760 | tf_op jit(solution)/shard_map/broadcast_in_dim;reshape | solution.py:144
  258.1 6.3 %all-to-all-start = ((f32[1,1024,1280]{2,0,1:T(1,128)}), f32[1,1024,1280]{2,0,1:T(1,128)}, u32[]{:S(2)}, u32[]{:S(2)}) async-start(f32[1,1024,1280]{2,0,1:T(1,128)} %copy.167), calls=%async_computation.3 | async-start | bytes 10485760 | tf_op jit(solution)/shard_map/all_to_all | solution.py:144
  279.3 2.6 broadcast_in_dim.99
  281.9 5.9 %copy.173 = f32[8,128,1280]{2,1,0:T(8,128)} copy(f32[8,128,1280]{1,2,0:T(8,128)} %bitcast.102) | data formatting | bytes 10485760 | tf_op jit(solution)/shard_map/reshape | solution.py:149
  287.8 83.8 %all-to-all-done = f32[1,1024,1280]{2,0,1:T(1,128)} async-done(((f32[1,1024,1280]{2,0,1:T(1,128)}), f32[1,1024,1280]{2,0,1:T(1,128)}, u32[]{:S(2)}, u32[]{:S(2)}) %all-to-all-start) | async-done | bytes 5242912 | tf_op jit(solution)/shard_map/all_to_all | solution.py:144
  371.6 3.0 copy.202
  (160 shorter events, 69.8 us)
Async XLA Ops:
  6.5 1.0 copy-start
  6.5 38.2 %reduce-scatter.6.cloned.1.call-start = ((), (), s32[]{:S(2)}) async-start(), calls=%async_computation.7 | async-start | bytes 1966080 | tf_op jit(solution)/shard_map/reduce_scatter | solution.py:96
  19.6 50.7 %reduce-scatter.4.cloned.1.call-start = ((), (), s32[]{:S(2)}) async-start(), calls=%async_computation.6 | async-start | bytes 1966080 | tf_op jit(solution)/shard_map/reduce_scatter | solution.py:95
  24.6 89.4 %reduce-scatter.8.cloned.1.call-start = ((), (), s32[]{:S(2)}) async-start(), calls=%async_computation.8 | async-start | bytes 1966080 | tf_op jit(solution)/shard_map/reduce_scatter | solution.py:97
  75.3 65.4 %copy-start.3 = (bf16[128,1280]{1,0:T(8,128)(2,1)}, bf16[128,1280]{1,0:T(8,128)(2,1)S(1)}, u32[]{:S(2)}) copy-start(bf16[128,1280]{1,0:T(8,128)(2,1)S(1)} %get-tuple-element.237) | copy-start | bytes 983044
  75.3 12.0 %collective-permute-start = (bf16[128,1280]{1,0:T(8,128)(2,1)S(1)}, bf16[128,1280]{1,0:T(8,128)(2,1)S(1)}, u32[]{:S(2)}, u32[]{:S(2)}) collective-permute-start(bf16[128,1280]{1,0:T(8,128)(2,1)S(1)} %get-tuple-element.236), channel_id=1, source_target_pairs={{0,2},{2,4},{4,6},{6,8},{8,10},{10,12},{12,14},{14,0},{1,3},{3,5},... | collective-permute-start | bytes 983048 | tf_op jit(solution)/shard_map/ppermute | solution.py:121
  87.4 21.4 %copy-start.6 = (bf16[128,1280]{1,0:T(8,128)(2,1)}, bf16[128,1280]{1,0:T(8,128)(2,1)S(1)}, u32[]{:S(2)}) copy-start(bf16[128,1280]{1,0:T(8,128)(2,1)S(1)} %collective-permute-done) | copy-start | bytes 983044
  87.4 11.1 %collective-permute-start.1 = (bf16[128,1280]{1,0:T(8,128)(2,1)S(1)}, bf16[128,1280]{1,0:T(8,128)(2,1)S(1)}, u32[]{:S(2)}, u32[]{:S(2)}) collective-permute-start(bf16[128,1280]{1,0:T(8,128)(2,1)S(1)} %collective-permute-done), channel_id=1, source_target_pairs={{0,2},{2,4},{4,6},{6,8},{8,10},{10,12},{12,14},{14,0},{1,3},{3,5},... | collective-permute-start | bytes 983048 | tf_op jit(solution)/shard_map/ppermute | solution.py:121
  98.5 10.3 %copy-start.8 = (bf16[128,1280]{1,0:T(8,128)(2,1)}, bf16[128,1280]{1,0:T(8,128)(2,1)S(1)}, u32[]{:S(2)}) copy-start(bf16[128,1280]{1,0:T(8,128)(2,1)S(1)} %collective-permute-done.1) | copy-start | bytes 983044
  98.5 10.3 %collective-permute-start.2 = (bf16[128,1280]{1,0:T(8,128)(2,1)S(1)}, bf16[128,1280]{1,0:T(8,128)(2,1)S(1)}, u32[]{:S(2)}, u32[]{:S(2)}) collective-permute-start(bf16[128,1280]{1,0:T(8,128)(2,1)S(1)} %collective-permute-done.1), channel_id=1, source_target_pairs={{0,2},{2,4},{4,6},{6,8},{8,10},{10,12},{12,14},{14,0},{1,3},{3,5},... | collective-permute-start | bytes 983048 | tf_op jit(solution)/shard_map/ppermute | solution.py:121
  108.7 9.9 %copy-start.10 = (bf16[128,1280]{1,0:T(8,128)(2,1)}, bf16[128,1280]{1,0:T(8,128)(2,1)S(1)}, u32[]{:S(2)}) copy-start(bf16[128,1280]{1,0:T(8,128)(2,1)S(1)} %collective-permute-done.2) | copy-start | bytes 983044
  108.7 9.9 %collective-permute-start.3 = (bf16[128,1280]{1,0:T(8,128)(2,1)S(1)}, bf16[128,1280]{1,0:T(8,128)(2,1)}, u32[]{:S(2)}, u32[]{:S(2)}) collective-permute-start(bf16[128,1280]{1,0:T(8,128)(2,1)S(1)} %collective-permute-done.2), channel_id=1, source_target_pairs={{0,2},{2,4},{4,6},{6,8},{8,10},{10,12},{12,14},{14,0},{1,3},{3,5},... | collective-permute-start | bytes 983048 | tf_op jit(solution)/shard_map/ppermute | solution.py:121
  108.8 9.9 %collective-permute-start.7 = (bf16[128,1280]{1,0:T(8,128)(2,1)S(1)}, bf16[128,1280]{1,0:T(8,128)(2,1)}, u32[]{:S(2)}, u32[]{:S(2)}) collective-permute-start(bf16[128,1280]{1,0:T(8,128)(2,1)S(1)} %get-tuple-element.237), channel_id=1, source_target_pairs={{0,16},{1,17},{2,18},{3,19},{4,20},{5,21},{6,22},{7,23},{8,24},{9,... | collective-permute-start | bytes 983048 | tf_op jit(solution)/shard_map/ppermute | solution.py:16
  115.9 12.8 %collective-permute-start.8 = (bf16[128,1280]{1,0:T(8,128)(2,1)}, bf16[128,1280]{1,0:T(8,128)(2,1)}, u32[]{:S(2)}, u32[]{:S(2)}) collective-permute-start(bf16[128,1280]{1,0:T(8,128)(2,1)} %convert_element_type.57), channel_id=1, source_target_pairs={{0,16},{1,17},{2,18},{3,19},{4,20},{5,21},{6,22},{7,23},{8,24},{9,... | collective-permute-start | bytes 983048 | tf_op jit(solution)/shard_map/ppermute | solution.py:16
  118.6 10.1 %collective-permute-start.4 = (bf16[128,1280]{1,0:T(8,128)(2,1)}, bf16[128,1280]{1,0:T(8,128)(2,1)}, u32[]{:S(2)}, u32[]{:S(2)}) collective-permute-start(bf16[128,1280]{1,0:T(8,128)(2,1)} %collective-permute-done.3), channel_id=1, source_target_pairs={{0,2},{2,4},{4,6},{6,8},{8,10},{10,12},{12,14},{14,0},{1,3},{3,5},... | collective-permute-start | bytes 983048 | tf_op jit(solution)/shard_map/ppermute | solution.py:121
  128.7 10.4 %collective-permute-start.5 = (bf16[128,1280]{1,0:T(8,128)(2,1)}, bf16[128,1280]{1,0:T(8,128)(2,1)}, u32[]{:S(2)}, u32[]{:S(2)}) collective-permute-start(bf16[128,1280]{1,0:T(8,128)(2,1)} %collective-permute-done.4), channel_id=1, source_target_pairs={{0,2},{2,4},{4,6},{6,8},{8,10},{10,12},{12,14},{14,0},{1,3},{3,5},... | collective-permute-start | bytes 983048 | tf_op jit(solution)/shard_map/ppermute | solution.py:121
  130.6 23.1 %copy-start.7 = (bf16[128,1280]{1,0:T(8,128)(2,1)S(1)}, bf16[128,1280]{1,0:T(8,128)(2,1)}, u32[]{:S(2)}) copy-start(bf16[128,1280]{1,0:T(8,128)(2,1)} %copy-done.6) | copy-start | bytes 983044
  139.1 10.5 %collective-permute-start.6 = (bf16[128,1280]{1,0:T(8,128)(2,1)}, bf16[128,1280]{1,0:T(8,128)(2,1)}, u32[]{:S(2)}, u32[]{:S(2)}) collective-permute-start(bf16[128,1280]{1,0:T(8,128)(2,1)} %collective-permute-done.5), channel_id=1, source_target_pairs={{0,2},{2,4},{4,6},{6,8},{8,10},{10,12},{12,14},{14,0},{1,3},{3,5},... | collective-permute-start | bytes 983048 | tf_op jit(solution)/shard_map/ppermute | solution.py:121
  140.8 12.9 %copy-start.11 = (bf16[128,1280]{1,0:T(8,128)(2,1)S(1)}, bf16[128,1280]{1,0:T(8,128)(2,1)}, u32[]{:S(2)}) copy-start(bf16[128,1280]{1,0:T(8,128)(2,1)} %copy-done.10) | copy-start | bytes 983044
  140.8 12.9 %copy-start.9 = (bf16[128,1280]{1,0:T(8,128)(2,1)S(1)}, bf16[128,1280]{1,0:T(8,128)(2,1)}, u32[]{:S(2)}) copy-start(bf16[128,1280]{1,0:T(8,128)(2,1)} %copy-done.8) | copy-start | bytes 983044
  172.8 9.3 %copy-start.5 = (bf16[512,1280]{0,1:T(8,128)(2,1)S(1)}, bf16[512,1280]{0,1:T(8,128)(2,1)}, u32[]{:S(2)}) copy-start(bf16[512,1280]{0,1:T(8,128)(2,1)} %get-tuple-element.361) | copy-start | bytes 3932164 | tf_op jit(solution)/shard_map/while
  208.3 9.3 %copy-start.5 = (bf16[512,1280]{0,1:T(8,128)(2,1)S(1)}, bf16[512,1280]{0,1:T(8,128)(2,1)}, u32[]{:S(2)}) copy-start(bf16[512,1280]{0,1:T(8,128)(2,1)} %get-tuple-element.361) | copy-start | bytes 3932164 | tf_op jit(solution)/shard_map/while
  234.2 10.4 %all-to-all-start.1 = ((f32[8,1,2048]{2,1,0:T(1,128)}), f32[8,1,2048]{2,1,0:T(1,128)S(1)}, u32[]{:S(2)}, u32[]{:S(2)}) async-start(f32[8,1,2048]{2,1,0:T(1,128)} %reshape.390), calls=%async_computation.4 | async-start | bytes 131072 | tf_op jit(solution)/shard_map/all_to_all | solution.py:142
  244.6 13.5 %all-to-all-start.2 = ((f32[8,1,2048]{2,1,0:T(1,128)}), f32[8,1,2048]{2,1,0:T(1,128)S(1)}, u32[]{:S(2)}, u32[]{:S(2)}) async-start(f32[8,1,2048]{2,1,0:T(1,128)} %reshape.392), calls=%async_computation.5 | async-start | bytes 131072 | tf_op jit(solution)/shard_map/all_to_all | solution.py:143
  258.1 6.4 %copy-start.4 = (bf16[128,1280]{1,0:T(8,128)(2,1)S(1)}, bf16[128,1280]{1,0:T(8,128)(2,1)}, u32[]{:S(2)}) copy-start(bf16[128,1280]{1,0:T(8,128)(2,1)} %copy-done.3) | copy-start | bytes 983044
  258.1 113.5 %all-to-all-start = ((f32[1,1024,1280]{2,0,1:T(1,128)}), f32[1,1024,1280]{2,0,1:T(1,128)}, u32[]{:S(2)}, u32[]{:S(2)}) async-start(f32[1,1024,1280]{2,0,1:T(1,128)} %copy.167), calls=%async_computation.3 | async-start | bytes 10485760 | tf_op jit(solution)/shard_map/all_to_all | solution.py:144
  371.6 4.0 %copy-start.2 = (f32[8,128,1280]{2,1,0:T(8,128)S(1)}, f32[8,128,1280]{2,1,0:T(8,128)}, u32[]{:S(2)}) copy-start(f32[8,128,1280]{2,1,0:T(8,128)} %copy.173) | copy-start | bytes 15728644
  374.5 2.9 copy-start.1
Sparse Core Ops, SparseCore 0:
  19.7 25.0 reduce-scatter.5
  47.0 23.2 reduce-scatter.3
  72.6 23.2 reduce-scatter.7
